TPU v7x, 256 devices: a whole 4x4x8 slice. The times are simulated.
256 devices in a mesh: lon: 32 (over y, z), lat: 8 (over x, core).
Axes of the slice: x: 4, y: 4, z: 8, core: 2. Of those that a mesh axis runs over, the one named last changes fastest.
Arguments:
- fields: float32 [129, 6, 128, 1024], P(None, None, 'lat', 'lon'), may hold values from -38 to 38
Outputs:
- koopman_modes: float32 [30, 128, 1024, 128], P(None, 'lat', 'lon')
- forward_operator: float32 [128, 128], replicated
- backward_operator: float32 [128, 128], replicated
All inputs are finite; a program needn't handle non-finite values.
Results may differ from a plain program's by a relative error of at most 0.0001.
Values sent between devices are 32-bit elements; how exact they have to be, the bound alone decides.
A program may use at most 64 MiB of HBM per device.

v0:
```python
import jax
import jax.numpy as jnp
from jax import lax
from jax.sharding import PartitionSpec as P


def with_halo(block, sides, width, periodic):
    for axis, dim in sides:
        count = lax.axis_size(axis)
        forward = [(i, i + 1) for i in range(count - 1)]
        if periodic:
            forward.append((count - 1, 0))
        backward = [(target, source) for source, target in forward]
        low = lax.ppermute(
            lax.slice_in_dim(block, block.shape[dim] - width, None, axis=dim), axis, forward
        )
        high = lax.ppermute(lax.slice_in_dim(block, 0, width, axis=dim), axis, backward)
        block = jnp.concatenate([low, block, high], axis=dim)
    return block


def reduced_operators(upper_factor, gram_total):
    snap_count = upper_factor.shape[0] - 1
    head_block = upper_factor[:snap_count, :snap_count]
    forward_operator = jax.scipy.linalg.solve_triangular(
        head_block.T, upper_factor[:snap_count, 1:].T, lower=True
    ).T
    back_factor = jnp.linalg.cholesky(gram_total[1:, 1:])
    mixed_block = jax.scipy.linalg.solve_triangular(
        back_factor, gram_total[1:, :snap_count], lower=True
    )
    backward_operator = jax.scipy.linalg.solve_triangular(back_factor, mixed_block.T, lower=True).T
    return (forward_operator, backward_operator)


def shards(fields):
    states = fields.shape[0]
    snap_count = states - 1
    channels = fields.shape[1]
    band_rows = fields.shape[2]
    sector_cols = fields.shape[3]
    lon_padded = with_halo(fields, (("lon", 3),), 1, True)
    lat_padded = with_halo(fields, (("lat", 2),), 1, False)
    neighbour_list = (
        lat_padded[:, :, :-2],
        lat_padded[:, :, 2:],
        lon_padded[:, :, :, :-2],
        lon_padded[:, :, :, 2:],
    )
    slab_list = [fields] + [fields * neighbour for neighbour in neighbour_list]
    rows_total = (
        5 * channels * band_rows * lax.axis_size("lat") * sector_cols * lax.axis_size("lon")
    )
    gram_local = jnp.zeros((states, states), jnp.float32)
    for feature_slab in slab_list:
        flat_rows = feature_slab.reshape(states, -1)
        gram_local = gram_local + jnp.dot(flat_rows, flat_rows.T, precision=lax.Precision.HIGHEST)
    gram_local = gram_local / rows_total
    gram_total = lax.psum(gram_local, ("lon", "lat"))
    upper_factor = jnp.linalg.cholesky(gram_total).T
    forward_operator, backward_operator = reduced_operators(upper_factor, gram_total)
    head_block = upper_factor[:snap_count, :snap_count]
    mode_parts = []
    for feature_slab in slab_list:
        flat_rows = feature_slab.reshape(states, -1)[:snap_count]
        solved = jax.scipy.linalg.solve_triangular(head_block.T, flat_rows, lower=True)
        mode_parts.append(
            solved.reshape(snap_count, channels, band_rows, sector_cols).transpose(1, 2, 3, 0)
        )
    koopman_modes = jnp.concatenate(mode_parts, axis=0)
    return (koopman_modes, forward_operator, backward_operator)


def solution(mesh):
    placed = (P(None, None, "lat", "lon"),)
    return jax.shard_map(
        shards,
        mesh=mesh,
        in_specs=placed,
        out_specs=(P(None, "lat", "lon", None), P(), P()),
        check_vma=False,
    )
```

profile of v0, /device:TPU:1, one launch (start us, length us, event | category | flops | bytes accessed | tf_op | source)
XLA Modules:
  0.0 388.6 jit_solution(6079797568631075508)
XLA Ops:
  7.2 1.5 fusion.35
  8.8 8.9 %collective-permute-start.3 = (f32[129,6,16,1]{0,2,3,1:T(8,128)S(1)}, f32[129,6,16,1]{0,2,3,1:T(8,128)S(1)}, u32[]{:S(2)}, u32[]{:S(2)}) collective-permute-start(f32[129,6,16,1]{0,2,3,1:T(8,128)S(1)} %copy.74), channel_id=1, source_target_pairs={{8,0},{16,8},{24,16},{32,24},{40,32},{48,40},{56,48},{64,56},{72,6... | collective-permute-start | bytes 148616 | tf_op jit(solution)/shard_map/ppermute | solution.py:17
  17.8 1.1 fusion.34
  18.8 4.0 %collective-permute-start = (f32[129,6,1,32]{0,3,2,1:T(8,128)S(1)}, f32[129,6,1,32]{0,3,2,1:T(8,128)S(1)}, u32[]{:S(2)}, u32[]{:S(2)}) collective-permute-start(f32[129,6,1,32]{0,3,2,1:T(8,128)S(1)} %get-tuple-element.18), channel_id=1, source_target_pairs={{0,1},{1,2},{2,3},{3,4},{4,5},{5,6},{6,7},{8,9},{9,10},{10,11},{11... | collective-permute-start | bytes 297224 | tf_op jit(solution)/shard_map/ppermute | solution.py:14
  22.8 2.2 collective-permute-start.1
  25.0 8.0 %convolution_bitcast_fusion.4 = f32[129,129]{0,1:T(8,128)S(1)} fusion(f32[129,6,16,32]{0,3,2,1:T(8,128)} %param.5), kind=kOutput, calls=%fused_computation.12 | convolution fusion | flops 613453824 | bytes 1651716 | tf_op jit(solution)/shard_map/dot_general | solution.py:57
  33.3 2.5 fusion.3
  35.8 5.1 %convolution_bitcast_fusion.2 = f32[129,129]{0,1:T(8,128)S(1)} fusion(f32[129,6,16,32]{0,3,2,1:T(8,128)S(1)} %get-tuple-element.15), kind=kOutput, calls=%fused_computation.10 | convolution fusion | flops 613453824 | bytes 1651716 | tf_op jit(solution)/shard_map/dot_general | solution.py:57
  41.0 5.1 %convolution_bitcast_fusion.1 = f32[129,129]{0,1:T(8,128)S(1)} fusion(f32[129,6,16,32]{0,3,2,1:T(8,128)S(1)} %get-tuple-element.16), kind=kOutput, calls=%fused_computation.9 | convolution fusion | flops 613453824 | bytes 1651716 | tf_op jit(solution)/shard_map/dot_general | solution.py:57
  46.1 5.3 %convolution_bitcast_fusion = f32[129,129]{0,1:T(8,128)S(1)} fusion(f32[129,6,16,32]{0,3,2,1:T(8,128)S(1)} %get-tuple-element.17), kind=kOutput, calls=%fused_computation.8 | convolution fusion | flops 613453824 | bytes 1651716 | tf_op jit(solution)/shard_map/dot_general | solution.py:57
  51.5 5.8 %fusion.8 = f32[129,129]{0,1:T(8,128)} fusion(f32[129,129]{0,1:T(8,128)S(1)} %convolution_bitcast_fusion, f32[129,129]{0,1:T(8,128)S(1)} %convolution_bitcast_fusion.1, f32[129,129]{0,1:T(8,128)S(1)} %convolution_bitcast_fusion.2, f32[129,129]{0,1:T(8,128)S(1)} %convolution_bitcast_fusion.4, f32[129,6,16,32]{0,3,2,1:T(8,128)S(1)} %get-tuple-element.14), kind=kOutput, calls=%fused_computation.17 | convolution fusion | flops 613537024 | bytes 1917972 | tf_op jit(solution)/shard_map/dot_general | solution.py:57
  57.4 1.7 slice.141
  59.0 0.7 copy-done.4
  59.9 0.8 copy-done.2
  60.7 1.3 slice.143
  62.0 1.3 slice.140
  63.3 239.0 %all-reduce.3.cloned.1.call-done = f32[129,129]{0,1:T(8,128)} async-done(((f32[129,129]{0,1:T(8,128)}), f32[129,129]{0,1:T(8,128)}) %all-reduce.3.cloned.1.call-update) | async-done | bytes 66580 | tf_op jit(solution)/shard_map/psum | solution.py:59
  302.3 1.0 copy.45
  303.3 0.9 fusion.9
  304.2 0.5 cholesky.153
  304.8 1.0 slice.145
  305.9 1.0 fusion.16
  306.9 11.7 %cholesky.144 = f32[128,128]{1,0:T(8,128)S(1)} custom-call(f32[128,128]{1,0:T(8,128)S(1)} %fusion.16), custom_call_target="Cholesky" | custom-call | tf_op jit(solution)/shard_map/jit(cholesky)/cholesky | solution.py:28
  318.7 0.6 compare_reduce_fusion
  319.3 0.7 fusion.10
  320.0 10.2 %custom-call.31 = f32[1,128,128]{1,2,0:T(8,128)S(1)} custom-call(f32[1,128,128]{2,1,0:T(8,128)S(1)} %fusion.10), custom_call_target="InvertDiagBlocksLowerTriangular" | custom-call | tf_op jit(solution)/shard_map/jit(_solve_triangular)/triangular_solve | solution.py:32
  330.1 1.2 convolution_bitcast_fusion.6
  331.4 0.3 convolution_bitcast_fusion.5
  331.7 0.7 copy.55
  332.5 11.7 %cholesky.63 = f32[128,128]{1,0:T(8,128)S(1)} custom-call(f32[128,128]{1,0:T(8,128)S(1)} %copy.46), custom_call_target="Cholesky" | custom-call | tf_op jit(solution)/shard_map/jit(cholesky)/cholesky | solution.py:60
  344.2 0.7 compare_reduce_fusion.1
  345.0 9.8 %custom-call.17 = f32[1,128,128]{1,2,0:T(8,128)S(1)} custom-call(f32[1,128,128]{2,1,0:T(8,128)S(1)} %get-tuple-element.23), custom_call_target="InvertDiagBlocksLowerTriangular" | custom-call | tf_op jit(solution)/shard_map/jit(cholesky)/cholesky | solution.py:60
  354.8 0.8 fusion.33
  357.5 0.2 cholesky.140
  357.7 0.2 cholesky.141
  358.0 9.8 %custom-call.24 = f32[1,128,128]{1,2,0:T(8,128)S(1)} custom-call(f32[1,128,128]{2,1,0:T(8,128)S(1)} %fusion.13), custom_call_target="InvertDiagBlocksLowerTriangular" | custom-call | tf_op jit(solution)/shard_map/jit(_solve_triangular)/triangular_solve | solution.py:66
  367.9 0.3 convolution_bitcast_fusion.7
  368.2 0.7 copy.54
  368.9 2.8 fusion.24
  371.7 1.4 fusion.22
  373.1 1.4 fusion.20
  374.5 1.4 fusion.18
  375.9 1.4 fusion.26
  377.5 0.2 constant_dynamic-update-slice_fusion.3
  377.7 0.2 constant_dynamic-update-slice_fusion.2
  377.9 0.2 constant_dynamic-update-slice_fusion.1
  378.1 0.2 constant_dynamic-update-slice_fusion
  378.3 3.2 copy-done.9
  (41 shorter events, 1.2 us)
Async XLA Ops:
  7.2 295.1 %all-reduce.3.cloned.1.call-start = ((), (), s32[]{:S(2)}) async-start(), calls=%async_computation | async-start | bytes 278528 | tf_op jit(solution)/shard_map/psum | solution.py:59
  8.8 24.3 %collective-permute-start.3 = (f32[129,6,16,1]{0,2,3,1:T(8,128)S(1)}, f32[129,6,16,1]{0,2,3,1:T(8,128)S(1)}, u32[]{:S(2)}, u32[]{:S(2)}) collective-permute-start(f32[129,6,16,1]{0,2,3,1:T(8,128)S(1)} %copy.74), channel_id=1, source_target_pairs={{8,0},{16,8},{24,16},{32,24},{40,32},{48,40},{56,48},{64,56},{72,6... | collective-permute-start | bytes 148616 | tf_op jit(solution)/shard_map/ppermute | solution.py:17
  17.7 15.4 %collective-permute-start.2 = (f32[129,6,16,1]{0,2,3,1:T(8,128)S(1)}, f32[129,6,16,1]{0,2,3,1:T(8,128)S(1)}, u32[]{:S(2)}, u32[]{:S(2)}) collective-permute-start(f32[129,6,16,1]{0,2,3,1:T(8,128)S(1)} %copy.73), channel_id=1, source_target_pairs={{0,8},{8,16},{16,24},{24,32},{32,40},{40,48},{48,56},{56,64},{64,7... | collective-permute-start | bytes 148616 | tf_op jit(solution)/shard_map/ppermute | solution.py:14
  18.8 14.4 %collective-permute-start = (f32[129,6,1,32]{0,3,2,1:T(8,128)S(1)}, f32[129,6,1,32]{0,3,2,1:T(8,128)S(1)}, u32[]{:S(2)}, u32[]{:S(2)}) collective-permute-start(f32[129,6,1,32]{0,3,2,1:T(8,128)S(1)} %get-tuple-element.18), channel_id=1, source_target_pairs={{0,1},{1,2},{2,3},{3,4},{4,5},{5,6},{6,7},{8,9},{9,10},{10,11},{11... | collective-permute-start | bytes 297224 | tf_op jit(solution)/shard_map/ppermute | solution.py:14
  22.8 10.5 %copy-start = (f32[129,6,16,32]{0,3,2,1:T(8,128)S(1)}, f32[129,6,16,32]{0,3,2,1:T(8,128)}, u32[]{:S(2)}) copy-start(f32[129,6,16,32]{0,3,2,1:T(8,128)} %param.5) | copy-start | bytes 4755460
  22.8 10.4 %collective-permute-start.1 = (f32[129,6,1,32]{0,3,2,1:T(8,128)S(1)}, f32[129,6,1,32]{0,3,2,1:T(8,128)S(1)}, u32[]{:S(2)}, u32[]{:S(2)}) collective-permute-start(f32[129,6,1,32]{0,3,2,1:T(8,128)S(1)} %get-tuple-element.19), channel_id=1, source_target_pairs={{1,0},{2,1},{3,2},{4,3},{5,4},{6,5},{7,6},{9,8},{10,9},{11,10},{12... | collective-permute-start | bytes 297224 | tf_op jit(solution)/shard_map/ppermute | solution.py:17
  35.8 5.2 %copy-start.3 = (f32[129,6,16,32]{0,3,2,1:T(8,128)}, f32[129,6,16,32]{0,3,2,1:T(8,128)S(1)}, u32[]{:S(2)}) copy-start(f32[129,6,16,32]{0,3,2,1:T(8,128)S(1)} %get-tuple-element.16) | copy-start | bytes 4755460
  35.8 10.3 %copy-start.1 = (f32[129,6,16,32]{0,3,2,1:T(8,128)}, f32[129,6,16,32]{0,3,2,1:T(8,128)S(1)}, u32[]{:S(2)}) copy-start(f32[129,6,16,32]{0,3,2,1:T(8,128)S(1)} %get-tuple-element.17) | copy-start | bytes 4755460
  35.8 15.7 %copy-start.5 = (f32[129,6,16,32]{0,3,2,1:T(8,128)}, f32[129,6,16,32]{0,3,2,1:T(8,128)S(1)}, u32[]{:S(2)}) copy-start(f32[129,6,16,32]{0,3,2,1:T(8,128)S(1)} %get-tuple-element.15) | copy-start | bytes 4755460
  35.8 15.7 %copy-start.6 = (f32[129,6,16,32]{0,3,2,1:T(8,128)}, f32[129,6,16,32]{0,3,2,1:T(8,128)S(1)}, u32[]{:S(2)}) copy-start(f32[129,6,16,32]{0,3,2,1:T(8,128)S(1)} %get-tuple-element.14) | copy-start | bytes 4755460
  57.3 2.4 copy-start.4
  57.4 3.3 copy-start.2
  59.7 2.3 copy-start.7
  371.7 2.8 copy-start.8
  373.1 2.8 slice-start
  378.3 3.2 copy-start.9
Sparse Core Ops, SparseCore 0:
  57.5 244.7 all-reduce.2
where the time goes:
time: 394 us; the launch traced here: 389 us
  waiting for transfers between devices  239 us (61%)
  other arithmetic  59.7 us (15%)
  matrix products  40.3 us (10%)
  local copies, waits for them, and re-layouts  17.7 us (4%)
  between operations  16.6 us (4%)
  starting transfers between devices  15.2 us (4%)
    psum x1, waiting for transfers between devices, shards(): gram_total = lax.psum(gram_local, ('lon', 'lat'))  239 us
    dot_general x5, matrix products, shards(): jnp.dot(flat_rows, flat_rows.T, precision=lax.Precision.HIGHEST)  29.4 us
    another operation x4, other arithmetic, shards(): upper_factor = jnp.linalg.cholesky(gram_total).T  22.3 us
    another operation x3, other arithmetic, reduced_operators(): back_factor = jnp.linalg.cholesky(gram_total[1:, 1:])  12.4 us
    ppermute x2, starting transfers between devices, with_halo(): lax.ppermute(lax.slice_in_dim(block, 0, width, axis=dim), axis, backward)  11.1 us
    another operation x2, other arithmetic, reduced_operators(): jax.scipy.linalg.solve_triangular(back_factor, mixed_block.T, lower=True)  10.8 us
    another operation x2, other arithmetic, shards(): jax.scipy.linalg.solve_triangular(head_block.T, flat_rows, lower=True)  9.82 us
    another operation x5, matrix products, shards(): jax.scipy.linalg.solve_triangular(head_block.T, flat_rows, lower=True)  8.3 us
  transfers between devices with their start and end apart: 5, of which 1 were waited for; matrix products, arithmetic and copies ran while one was open for 4% of the time, Pallas kernels for 0%

commit v1 on v0

--- a/solution.py
+++ b/solution.py
@@ -56,7 +56,13 @@
         flat_rows = feature_slab.reshape(states, -1)
         gram_local = gram_local + jnp.dot(flat_rows, flat_rows.T, precision=lax.Precision.HIGHEST)
     gram_local = gram_local / rows_total
-    gram_total = lax.psum(gram_local, ("lon", "lat"))
+
+    def _update_flows(local_x, row_axis):
+        small = lax.all_gather(local_x, row_axis)
+        far_arr = jnp.sum(small, 0)
+        return far_arr
+
+    gram_total = _update_flows(gram_local, ("lon", "lat"))
     upper_factor = jnp.linalg.cholesky(gram_total).T
     forward_operator, backward_operator = reduced_operators(upper_factor, gram_total)
     head_block = upper_factor[:snap_count, :snap_count]

time: 394 us -> 334 us (0.85)
  waiting for transfers between devices: 239 us -> 149 us
  other arithmetic: 59.7 us -> 74.7 us
  matrix products: 40.3 us -> 53.3 us
    psum x1 -> x0, waiting for transfers between devices: 239 us -> none  [shards(): gram_total = lax.psum(gram_local, ('lon', 'lat'))]
    all_gather x0 -> x1, waiting for transfers between devices: none -> 149 us  [_update_flows(): small = lax.all_gather(local_x, row_axis)]
    dot_general x5, matrix products: 29.4 us -> 42.7 us  [shards(): jnp.dot(flat_rows, flat_rows.T, precision=lax.Precision.HIGHEST)]
    reduce_sum x0 -> x1, other arithmetic: none -> 12.5 us  [_update_flows(): far_arr = jnp.sum(small, 0)]
where the time goes in v1:
time: 334 us; the launch traced here: 328 us
  waiting for transfers between devices  149 us (45%)
  other arithmetic  74.7 us (22%)
  matrix products  53.3 us (16%)
  local copies, waits for them, and re-layouts  19.3 us (6%)
  between operations  16.9 us (5%)
  starting transfers between devices  15.2 us (5%)
    all_gather x1, waiting for transfers between devices, _update_flows(): small = lax.all_gather(local_x, row_axis)  149 us
    dot_general x5, matrix products, shards(): jnp.dot(flat_rows, flat_rows.T, precision=lax.Precision.HIGHEST)  42.7 us
    another operation x4, other arithmetic, shards(): upper_factor = jnp.linalg.cholesky(gram_total).T  26 us
    reduce_sum x1, other arithmetic, _update_flows(): far_arr = jnp.sum(small, 0)  12.5 us
    another operation x3, other arithmetic, reduced_operators(): back_factor = jnp.linalg.cholesky(gram_total[1:, 1:])  12.4 us
    ppermute x2, starting transfers between devices, with_halo(): lax.ppermute(lax.slice_in_dim(block, 0, width, axis=dim), axis, backward)  11.1 us
    another operation x2, other arithmetic, reduced_operators(): jax.scipy.linalg.solve_triangular(back_factor, mixed_block.T, lower=True)  10.5 us
    another operation x2, other arithmetic, shards(): jax.scipy.linalg.solve_triangular(head_block.T, flat_rows, lower=True)  9.82 us
  transfers between devices with their start and end apart: 5, of which 1 were waited for; matrix products, arithmetic and copies ran while one was open for 4% of the time, Pallas kernels for 0%

profile of v1, /device:TPU:1, one launch (start us, length us, event | category | flops | bytes accessed | tf_op | source)
XLA Modules:
  0.0 327.9 jit_solution(17309855305233095214)
XLA Ops:
  7.2 1.5 fusion.35
  8.8 8.9 %collective-permute-start.3 = (f32[129,6,16,1]{0,2,3,1:T(8,128)S(1)}, f32[129,6,16,1]{0,2,3,1:T(8,128)S(1)}, u32[]{:S(2)}, u32[]{:S(2)}) collective-permute-start(f32[129,6,16,1]{0,2,3,1:T(8,128)S(1)} %copy.53), channel_id=1, source_target_pairs={{8,0},{16,8},{24,16},{32,24},{40,32},{48,40},{56,48},{64,56},{72,6... | collective-permute-start | bytes 148616 | tf_op jit(solution)/shard_map/ppermute | solution.py:17
  17.8 1.1 fusion.34
  18.8 4.0 %collective-permute-start = (f32[129,6,1,32]{0,3,2,1:T(8,128)S(1)}, f32[129,6,1,32]{0,3,2,1:T(8,128)S(1)}, u32[]{:S(2)}, u32[]{:S(2)}) collective-permute-start(f32[129,6,1,32]{0,3,2,1:T(8,128)S(1)} %get-tuple-element.18), channel_id=1, source_target_pairs={{0,1},{1,2},{2,3},{3,4},{4,5},{5,6},{6,7},{8,9},{9,10},{10,11},{11... | collective-permute-start | bytes 297224 | tf_op jit(solution)/shard_map/ppermute | solution.py:14
  22.8 2.2 collective-permute-start.1
  25.0 8.0 %convolution_bitcast_fusion.4 = f32[129,129]{1,0:T(8,128)S(1)} fusion(f32[129,6,16,32]{0,3,2,1:T(8,128)} %param.5), kind=kOutput, calls=%fused_computation.12 | convolution fusion | flops 613453824 | bytes 1651716 | tf_op jit(solution)/shard_map/dot_general | solution.py:57
  33.3 2.6 fusion.3
  35.9 5.3 %convolution_bitcast_fusion.2 = f32[129,129]{1,0:T(8,128)S(1)} fusion(f32[129,6,16,32]{0,3,2,1:T(8,128)S(1)} %get-tuple-element.15), kind=kOutput, calls=%fused_computation.10 | convolution fusion | flops 613453824 | bytes 1651716 | tf_op jit(solution)/shard_map/dot_general | solution.py:57
  41.2 5.3 %convolution_bitcast_fusion.1 = f32[129,129]{1,0:T(8,128)S(1)} fusion(f32[129,6,16,32]{0,3,2,1:T(8,128)S(1)} %get-tuple-element.16), kind=kOutput, calls=%fused_computation.9 | convolution fusion | flops 613453824 | bytes 1651716 | tf_op jit(solution)/shard_map/dot_general | solution.py:57
  46.4 18.3 %convolution_bitcast_fusion = f32[129,129]{1,0:T(8,128)S(1)} fusion(f32[129,6,16,32]{0,3,2,1:T(8,128)S(1)} %get-tuple-element.17), kind=kOutput, calls=%fused_computation.8 | convolution fusion | flops 613453824 | bytes 1651716 | tf_op jit(solution)/shard_map/dot_general | solution.py:57
  64.7 5.9 %fusion.9 = f32[1,129,129]{2,1,0:T(8,128)} fusion(f32[129,129]{1,0:T(8,128)S(1)} %convolution_bitcast_fusion, f32[129,129]{1,0:T(8,128)S(1)} %convolution_bitcast_fusion.1, f32[129,129]{1,0:T(8,128)S(1)} %convolution_bitcast_fusion.2, f32[129,129]{1,0:T(8,128)S(1)} %convolution_bitcast_fusion.4, f32[129,6,16,32]{0,3,2,1:T(8,128)S(1)} %get-tuple-element.14), kind=kOutput, calls=%fused_computation.18 | convolution fusion | flops 613537024 | bytes 1917972 | tf_op jit(solution)/shard_map/dot_general | solution.py:57
  70.7 1.7 slice.141
  72.4 0.7 copy-done.4
  73.2 0.8 copy-done.2
  74.0 1.3 slice.143
  75.3 1.3 slice.140
  76.6 148.6 %all-gather.4.cloned.1.call-done = f32[256,129,129]{2,1,0:T(8,128)} async-done(((f32[1,129,129]{2,1,0:T(8,128)}), f32[256,129,129]{2,1,0:T(8,128)}) %all-gather.4.cloned.1.call-update) | async-done | bytes 17040400 | tf_op jit(solution)/shard_map/all_gather | solution.py:61
  225.2 12.5 %reduce_sum.9 = f32[129,129]{1,0:T(8,128)S(1)} reduce(f32[256,129,129]{2,1,0:T(8,128)} %all-gather.4.cloned.1.call-done, f32[]{:T(128)} %constant.99.clone.1), dimensions={0}, to_apply=%region_0.0 | reduce | flops 4243455 | bytes 17106952 | tf_op jit(solution)/shard_map/reduce_sum | solution.py:62
  237.9 0.6 cholesky.153
  238.5 0.6 cholesky.152
  239.2 12.5 %cholesky.63 = f32[128,128]{1,0:T(8,128)S(1)} custom-call(f32[128,128]{1,0:T(8,128)} %cholesky.152), custom_call_target="Cholesky" | custom-call | tf_op jit(solution)/shard_map/jit(cholesky)/cholesky | solution.py:66
  251.7 1.2 select_reduce_fusion.1
  252.9 0.7 cholesky.138
  253.8 11.7 %cholesky.144 = f32[128,128]{1,0:T(8,128)S(1)} custom-call(f32[128,128]{1,0:T(8,128)S(1)} %fusion.17), custom_call_target="Cholesky" | custom-call | tf_op jit(solution)/shard_map/jit(cholesky)/cholesky | solution.py:28
  265.5 0.6 compare_reduce_fusion
  266.2 0.7 fusion.11
  266.9 9.8 %custom-call.31 = f32[1,128,128]{1,2,0:T(8,128)S(1)} custom-call(f32[1,128,128]{2,1,0:T(8,128)S(1)} %fusion.11), custom_call_target="InvertDiagBlocksLowerTriangular" | custom-call | tf_op jit(solution)/shard_map/jit(_solve_triangular)/triangular_solve | solution.py:32
  276.7 0.3 convolution_bitcast_fusion.6
  277.0 0.3 convolution_bitcast_fusion.5
  277.3 0.7 copy.39
  278.0 1.4 compare_reduce_fusion.1
  279.4 10.8 %custom-call.17 = f32[1,128,128]{1,2,0:T(8,128)S(1)} custom-call(f32[1,128,128]{2,1,0:T(8,128)} %get-tuple-element.23), custom_call_target="InvertDiagBlocksLowerTriangular" | custom-call | tf_op jit(solution)/shard_map/jit(cholesky)/cholesky | solution.py:66
  290.2 1.4 fusion.33
  292.9 1.3 cholesky.140
  294.2 1.3 cholesky.141
  296.2 0.9 select_bitcast_fusion
  297.2 9.8 %custom-call.24 = f32[1,128,128]{1,2,0:T(8,128)S(1)} custom-call(f32[1,128,128]{2,1,0:T(8,128)S(1)} %fusion.14), custom_call_target="InvertDiagBlocksLowerTriangular" | custom-call | tf_op jit(solution)/shard_map/jit(_solve_triangular)/triangular_solve | solution.py:72
  307.0 0.3 convolution_bitcast_fusion.7
  307.3 0.7 copy.38
  308.0 2.8 fusion.25
  310.8 1.4 fusion.23
  312.2 1.4 fusion.21
  313.6 1.4 fusion.19
  315.0 1.4 fusion.27
  316.6 0.2 constant_dynamic-update-slice_fusion.3
  316.8 0.2 constant_dynamic-update-slice_fusion.2
  317.0 0.2 constant_dynamic-update-slice_fusion.1
  317.4 3.2 copy-done.9
  (42 shorter events, 1.5 us)
Async XLA Ops:
  7.2 218.0 %all-gather.4.cloned.1.call-start = ((), (), s32[]{:S(2)}) async-start(), calls=%async_computation | async-start | bytes 35790848 | tf_op jit(solution)/shard_map/all_gather | solution.py:61
  8.8 24.2 %collective-permute-start.3 = (f32[129,6,16,1]{0,2,3,1:T(8,128)S(1)}, f32[129,6,16,1]{0,2,3,1:T(8,128)S(1)}, u32[]{:S(2)}, u32[]{:S(2)}) collective-permute-start(f32[129,6,16,1]{0,2,3,1:T(8,128)S(1)} %copy.53), channel_id=1, source_target_pairs={{8,0},{16,8},{24,16},{32,24},{40,32},{48,40},{56,48},{64,56},{72,6... | collective-permute-start | bytes 148616 | tf_op jit(solution)/shard_map/ppermute | solution.py:17
  17.7 15.4 %collective-permute-start.2 = (f32[129,6,16,1]{0,2,3,1:T(8,128)S(1)}, f32[129,6,16,1]{0,2,3,1:T(8,128)S(1)}, u32[]{:S(2)}, u32[]{:S(2)}) collective-permute-start(f32[129,6,16,1]{0,2,3,1:T(8,128)S(1)} %copy.52), channel_id=1, source_target_pairs={{0,8},{8,16},{16,24},{24,32},{32,40},{40,48},{48,56},{56,64},{64,7... | collective-permute-start | bytes 148616 | tf_op jit(solution)/shard_map/ppermute | solution.py:14
  18.8 14.4 %collective-permute-start = (f32[129,6,1,32]{0,3,2,1:T(8,128)S(1)}, f32[129,6,1,32]{0,3,2,1:T(8,128)S(1)}, u32[]{:S(2)}, u32[]{:S(2)}) collective-permute-start(f32[129,6,1,32]{0,3,2,1:T(8,128)S(1)} %get-tuple-element.18), channel_id=1, source_target_pairs={{0,1},{1,2},{2,3},{3,4},{4,5},{5,6},{6,7},{8,9},{9,10},{10,11},{11... | collective-permute-start | bytes 297224 | tf_op jit(solution)/shard_map/ppermute | solution.py:14
  22.8 10.5 %copy-start = (f32[129,6,16,32]{0,3,2,1:T(8,128)S(1)}, f32[129,6,16,32]{0,3,2,1:T(8,128)}, u32[]{:S(2)}) copy-start(f32[129,6,16,32]{0,3,2,1:T(8,128)} %param.5) | copy-start | bytes 4755460
  22.8 10.4 %collective-permute-start.1 = (f32[129,6,1,32]{0,3,2,1:T(8,128)S(1)}, f32[129,6,1,32]{0,3,2,1:T(8,128)S(1)}, u32[]{:S(2)}, u32[]{:S(2)}) collective-permute-start(f32[129,6,1,32]{0,3,2,1:T(8,128)S(1)} %get-tuple-element.19), channel_id=1, source_target_pairs={{1,0},{2,1},{3,2},{4,3},{5,4},{6,5},{7,6},{9,8},{10,9},{11,10},{12... | collective-permute-start | bytes 297224 | tf_op jit(solution)/shard_map/ppermute | solution.py:17
  35.8 5.3 %copy-start.3 = (f32[129,6,16,32]{0,3,2,1:T(8,128)}, f32[129,6,16,32]{0,3,2,1:T(8,128)S(1)}, u32[]{:S(2)}) copy-start(f32[129,6,16,32]{0,3,2,1:T(8,128)S(1)} %get-tuple-element.16) | copy-start | bytes 4755460
  35.8 10.6 %copy-start.1 = (f32[129,6,16,32]{0,3,2,1:T(8,128)}, f32[129,6,16,32]{0,3,2,1:T(8,128)S(1)}, u32[]{:S(2)}) copy-start(f32[129,6,16,32]{0,3,2,1:T(8,128)S(1)} %get-tuple-element.17) | copy-start | bytes 4755460
  35.9 28.8 %copy-start.5 = (f32[129,6,16,32]{0,3,2,1:T(8,128)}, f32[129,6,16,32]{0,3,2,1:T(8,128)S(1)}, u32[]{:S(2)}) copy-start(f32[129,6,16,32]{0,3,2,1:T(8,128)S(1)} %get-tuple-element.15) | copy-start | bytes 4755460
  35.9 28.8 %copy-start.6 = (f32[129,6,16,32]{0,3,2,1:T(8,128)}, f32[129,6,16,32]{0,3,2,1:T(8,128)S(1)}, u32[]{:S(2)}) copy-start(f32[129,6,16,32]{0,3,2,1:T(8,128)S(1)} %get-tuple-element.14) | copy-start | bytes 4755460
  70.7 2.4 copy-start.4
  70.7 3.3 %copy-start.2 = (f32[129,6,16,32]{0,3,2,1:T(8,128)S(1)}, f32[129,6,16,32]{0,3,2,1:T(8,128)}, u32[]{:S(2)}) copy-start(f32[129,6,16,32]{0,3,2,1:T(8,128)} %copy-done.1) | copy-start | bytes 4755460
  73.0 2.3 copy-start.7
  237.9 0.7 copy-start.10
  310.8 2.8 copy-start.8
  312.2 2.8 slice-start
  317.4 3.2 copy-start.9
Sparse Core Ops, SparseCore 0:
  70.8 154.3 all-gather.3
